TPU v7x, 256 devices: a whole 4x4x8 slice. The times are simulated.
256 devices in a mesh: grp: 16 (over x_lo, z), inner: 16 (over y, x_hi, core).
Axes of the slice: x: 4 (x_hi: 2, x_lo: 2; x = x_hi * 2 + x_lo), y: 4, z: 8, core: 2. Of those that a mesh axis runs over, the one named last changes fastest.
Arguments:
- signal: bfloat16 [128, 1024, 4096], P('grp', None, 'inner'), may hold values from -6 to 6
- bins: int32 [8], replicated, may hold values from 1 to 512, as said below
- mic_positions: float32 [3, 4096], replicated, may hold values from -1 to 1
- grid_positions: float32 [3, 1024], replicated, may hold values from 1 to 3
Outputs:
- beam_map: float32 [8, 1024], replicated
Inputs may be any that keep to these rules, and one draw needn't show every extreme that they name: The 8 bins are distinct; bin 1 and bin 1024 / 2 are always among them.
All inputs are finite; a program needn't handle non-finite values.
Results may differ from a plain program's by a relative error of at most 0.02.
Values may be sent and summed in bfloat16 or wider, within the bound.
A program may use at most 128 MiB of HBM per device.

v0:
```python
import math
import jax
import jax.numpy as jnp
from jax import lax
from jax.sharding import PartitionSpec as P

SAMPLES = 1024
F = 8
TWO_PI = 2.0 * math.pi
RATE_OVER_SOUND = 51200.0 / 343.0


def dft_table(bins):
    ticks = jnp.arange(SAMPLES, dtype=jnp.int32)
    turns = bins[:, None] * ticks[None, :] % SAMPLES
    angle = turns.astype(jnp.float32) * (TWO_PI / SAMPLES)
    window = 0.5 - 0.5 * jnp.cos(ticks.astype(jnp.float32) * (TWO_PI / SAMPLES))
    factor = math.sqrt(8.0 / (3.0 * SAMPLES))
    real_part = window[None, :] * jnp.cos(angle) * factor
    imag_part = -window[None, :] * jnp.sin(angle) * factor
    return jnp.concatenate([real_part, imag_part], 0).astype(jnp.bfloat16)


def distances(spots, grid):
    delta_x = grid[0][None, :] - spots[0][:, None]
    delta_y = grid[1][None, :] - spots[1][:, None]
    delta_z = grid[2][None, :] - spots[2][:, None]
    return jnp.sqrt(delta_x * delta_x + delta_y * delta_y + delta_z * delta_z) * RATE_OVER_SOUND


def steering(delay, frequency_bin):
    angle = delay * (frequency_bin.astype(jnp.float32) * (TWO_PI / SAMPLES))
    return jnp.concatenate([jnp.cos(angle), -jnp.sin(angle)], 0).astype(jnp.bfloat16)


def shards(signal, bins, mic_positions, grid_positions):
    table = dft_table(bins)
    local = jnp.einsum("kt,stm->skm", table, signal, preferred_element_type=jnp.float32).astype(
        jnp.bfloat16
    )
    snap_dev = local.shape[0]
    mic_cols = local.shape[2]
    local = local.reshape(snap_dev, 2, F, mic_cols)
    grp_size = lax.axis_size("grp")
    grp_index = lax.axis_index("grp")
    inner_index = lax.axis_index("inner")
    total_mics = mic_positions.shape[1]
    snaps = snap_dev * grp_size
    col_pos = lax.dynamic_slice_in_dim(mic_positions, inner_index * mic_cols, mic_cols, 1)
    col_delay = distances(col_pos, grid_positions)
    wide = lax.all_gather(local, "inner", axis=3, tiled=True)
    rows = lax.all_to_all(wide, "grp", split_axis=3, concat_axis=0, tiled=True)
    row_count = rows.shape[3]
    row_ids = grp_index * row_count + jnp.arange(row_count, dtype=jnp.int32)
    row_pos = lax.dynamic_slice_in_dim(mic_positions, grp_index * row_count, row_count, 1)
    col_ids = inner_index * mic_cols + jnp.arange(mic_cols, dtype=jnp.int32)
    row_delay = distances(row_pos, grid_positions)
    piece = lax.all_gather(local, "grp", axis=0, tiled=True)
    real_rows = rows[:, 0]
    imag_rows = rows[:, 1]
    real_cols = piece[:, 0]
    imag_cols = piece[:, 1]
    form = "sfm,sfn->fmn"
    real_sum = jnp.einsum(
        form, real_rows, real_cols, preferred_element_type=jnp.float32
    ) + jnp.einsum(form, imag_rows, imag_cols, preferred_element_type=jnp.float32)
    imag_sum = jnp.einsum(
        form, imag_rows, real_cols, preferred_element_type=jnp.float32
    ) - jnp.einsum(form, real_rows, imag_cols, preferred_element_type=jnp.float32)
    diagonal_mask = row_ids[:, None] == col_ids[None, :]
    partial_value = []
    for index in range(F):
        real_c = jnp.where(diagonal_mask, 0.0, real_sum[index] / snaps)
        imag_c = jnp.where(diagonal_mask, 0.0, imag_sum[index] / snaps)
        block = jnp.concatenate(
            [jnp.concatenate([real_c, -imag_c], 1), jnp.concatenate([imag_c, real_c], 1)], 0
        )
        col_steer = steering(col_delay, bins[index]).astype(jnp.float32)
        row_steer = steering(row_delay, bins[index]).astype(jnp.float32)
        image = jnp.dot(
            block, col_steer, precision=lax.Precision.HIGHEST, preferred_element_type=jnp.float32
        )
        partial_value.append(jnp.sum(row_steer * image, axis=0))
    partial_value = jnp.stack(partial_value, 0)
    total = lax.psum(partial_value, ("grp", "inner"))
    return total * (math.sqrt(snaps) / total_mics)


def solution(mesh):
    in_specs = (P("grp", None, "inner"), P(), P(), P())
    out_specs = P()
    return jax.shard_map(shards, mesh=mesh, in_specs=in_specs, out_specs=out_specs, check_vma=False)
```

profile of v0, /device:TPU:1, one launch (start us, length us, event | category | flops | bytes accessed | tf_op | source)
XLA Modules:
  0.0 348.1 jit_solution(14160871644973293209)
XLA Ops:
  6.6 0.9 multiply_convert_fusion.1
  7.5 3.5 fusion
  10.9 0.0 all-gather.3.cloned.1.call-update
  11.0 0.0 all-gather.5.cloned.1.call-start
  11.0 0.7 all-gather.5.cloned.1.call-update
  11.7 51.2 %all-gather.3.cloned.1.call-done = bf16[8,2,8,4096]{3,2,1,0:T(8,128)(2,1)} async-done(((bf16[8,2,8,256]{3,2,1,0:T(8,128)(2,1)}), bf16[8,2,8,4096]{3,2,1,0:T(8,128)(2,1)}) %all-gather.3.cloned.1.call-update) | async-done | bytes 1048592 | tf_op jit(solution)/shard_map/all_gather | solution.py:51
  62.9 32.9 %copy.11 = bf16[8,2,8,4096]{2,1,0,3:T(2,128)(2,1)} copy(bf16[8,2,8,4096]{3,2,1,0:T(8,128)(2,1)} %all-gather.3.cloned.1.call-done) | data formatting | bytes 2097152 | tf_op jit(solution)/shard_map/all_gather | solution.py:51
  95.8 20.6 %reshape.88 = bf16[16,2,16384]{2,1,0:T(2,128)(2,1)} reshape(bf16[4096,8,2,8]{3,2,1,0:T(2,128)(2,1)} %bitcast.129) | data formatting | bytes 2097152
  116.5 7.0 %all-to-all-start = ((bf16[16,2,16384]{2,1,0:T(2,128)(2,1)}), bf16[16,2,16384]{2,1,0:T(2,128)(2,1)S(1)}, u32[]{:S(2)}, u32[]{:S(2)}) async-start(bf16[16,2,16384]{2,1,0:T(2,128)(2,1)} %reshape.88), calls=%async_computation | async-start | bytes 2097152 | tf_op jit(solution)/shard_map/all_to_all | solution.py:52
  123.5 0.0 copy-done
  123.5 0.7 fusion.139
  129.3 0.9 constant_dynamic-slice_fusion.1
  130.2 66.2 %cosine_convert_fusion = (bf16[256,1024]{1,0:T(8,128)(2,1)}, bf16[256,1024]{1,0:T(8,128)(2,1)S(1)}, bf16[256,1024]{1,0:T(8,128)(2,1)}, bf16[256,1024]{1,0:T(8,12...) fusion(f32[]{:T(128)} %bitcast.49, ...), kind=kLoop, calls=%fused_computation.109 | loop fusion | flops 20971520 | bytes 16795680 | tf_op jit(solution)/shard_map/convert
  196.4 0.0 all-gather.5.cloned.1.call-done
  196.5 1.3 fusion.137
  197.7 0.4 copy.16
  198.2 0.4 copy.15
  198.6 0.0 all-to-all-done
  198.6 20.8 %reshape.89 = bf16[4096,8,2,8]{3,2,1,0:T(2,128)(2,1)} reshape(bf16[16,2,16384]{2,1,0:T(2,128)(2,1)S(1)} %all-to-all-done) | data formatting | bytes 2097152
  219.4 24.9 %copy.12 = bf16[8,2,8,16,256]{4,0,3,2,1:T(8,128)(2,1)S(1)} copy(bf16[8,2,8,16,256]{2,1,0,4,3:T(2,128)(2,1)} %bitcast.130) | data formatting | bytes 2097152 | tf_op jit(solution)/shard_map/all_to_all | solution.py:52
  244.3 0.4 fusion.83
  244.7 0.4 fusion.85
  245.1 0.4 convolution_add_fusion
  245.6 0.4 convolution_subtract_fusion
  246.0 0.0 copy-start.29
  246.0 0.0 copy-start.30
  246.0 0.0 copy-start.31
  246.0 0.0 copy-start.32
  246.1 0.8 fusion.129
  246.9 0.2 copy-done.29
  247.1 0.2 copy-done.30
  247.2 0.2 copy-done.31
  247.4 0.2 copy-done.32
  247.5 1.9 multiply_reduce_fusion.1
  249.5 0.0 copy-done.25
  249.5 0.0 copy-done.26
  249.5 0.0 copy-done.27
  249.5 0.0 copy-done.28
  249.5 0.0 copy-start.21
  249.5 0.0 copy-start.22
  249.6 0.0 copy-start.23
  249.6 0.0 copy-start.24
  249.6 1.9 multiply_reduce_fusion.2
  251.5 0.0 copy-done.21
  251.5 0.0 copy-done.22
  251.5 0.0 copy-done.23
  251.6 0.0 copy-done.24
  251.6 0.0 copy-start.17
  251.6 0.0 copy-start.18
  251.6 0.0 copy-start.19
  251.6 0.0 copy-start.20
  251.6 1.9 multiply_reduce_fusion.3
  253.6 0.0 copy-done.17
  253.6 0.0 copy-done.18
  253.6 0.0 copy-done.19
  253.6 0.0 copy-done.20
  253.6 1.9 multiply_reduce_fusion.4
  255.7 1.9 multiply_reduce_fusion.5
  257.7 2.2 multiply_reduce_fusion.6
  260.0 1.9 multiply_reduce_fusion
  261.9 1.9 multiply_reduce_fusion.7
  263.9 0.1 stack.35
  263.9 76.7 %psum.7 = f32[8,1024]{1,0:T(8,128)S(1)} all-reduce(f32[8,1024]{1,0:T(8,128)S(1)} %stack.35), channel_id=1, replica_groups=mesh['grp'=16,'inner'=16] {'grp','inner'}, use_global_device_ids=true, to_apply=%region_8.9 | all-reduce | flops 8192 | bytes 65536 | tf_op jit(solution)/shard_map/psum | solution.py:85
  340.6 0.6 broadcast_multiply_fusion
  (41 shorter events, 0.1 us)
Async XLA Ops:
  6.5 56.4 %all-gather.3.cloned.1.call-start = ((), (), s32[]{:S(2)}) async-start(), calls=%async_computation.1 | async-start | bytes 1114112 | tf_op jit(solution)/shard_map/all_gather | solution.py:51
  11.0 185.5 %all-gather.5.cloned.1.call-start = ((), (), s32[]{:S(2)}) async-start(), calls=%async_computation.2 | async-start | bytes 1114112 | tf_op jit(solution)/shard_map/all_gather | solution.py:58
  116.5 7.0 %copy-start = (s32[8]{0:T(128)S(1)}, s32[8]{0:T(128)}, u32[]{:S(2)}) copy-start(s32[8]{0:T(128)} %param.5) | copy-start | bytes 100
  116.5 13.7 %copy-start.1 = (f32[3,1024]{1,0:T(4,128)S(1)}, f32[3,1024]{1,0:T(4,128)}, u32[]{:S(2)}) copy-start(f32[3,1024]{1,0:T(4,128)} %param.7) | copy-start | bytes 36868
  116.5 82.2 %all-to-all-start = ((bf16[16,2,16384]{2,1,0:T(2,128)(2,1)}), bf16[16,2,16384]{2,1,0:T(2,128)(2,1)S(1)}, u32[]{:S(2)}, u32[]{:S(2)}) async-start(bf16[16,2,16384]{2,1,0:T(2,128)(2,1)} %reshape.88), calls=%async_computation | async-start | bytes 2097152 | tf_op jit(solution)/shard_map/all_to_all | solution.py:52
  246.0 1.0 copy-start.29
  246.0 1.2 copy-start.30
  246.0 1.3 copy-start.31
  246.0 1.5 copy-start.32
  247.5 2.0 copy-start.25
  247.5 2.0 copy-start.26
  247.5 2.0 copy-start.27
  247.5 2.0 copy-start.28
  249.5 2.0 copy-start.21
  249.5 2.0 copy-start.22
  249.6 2.0 copy-start.23
  249.6 2.0 copy-start.24
  251.6 2.0 copy-start.17
  251.6 2.0 copy-start.18
  251.6 2.0 copy-start.19
  251.6 2.0 copy-start.20
  253.6 2.0 copy-start.13
  253.6 2.0 copy-start.14
  253.6 2.0 copy-start.15
  253.6 2.0 copy-start.16
  255.6 2.0 copy-start.9
  255.6 2.0 copy-start.10
  255.6 2.0 copy-start.11
  255.6 2.0 copy-start.12
  257.6 2.2 copy-start.5
  257.7 2.2 copy-start.6
  257.7 2.2 copy-start.7
  257.7 2.2 copy-start.8
  259.9 2.0 copy-start.2
  259.9 2.0 copy-start.3
  259.9 2.0 copy-start.4
Sparse Core Ops, SparseCore 0:
  11.1 51.7 all-gather.2
  64.7 57.6 all-gather.4
where the time goes:
time: 353 us; the launch traced here: 348 us
  local copies, waits for them, and re-layouts  104 us (29%)
  blocking collectives  76.7 us (22%)
  other arithmetic  68.6 us (19%)
  waiting for transfers between devices  51.9 us (15%)
  matrix products  20.9 us (6%)
  between operations  19.1 us (5%)
  starting transfers between devices  7.02 us (2%)
    psum x1, blocking collectives, shards(): total = lax.psum(partial_value, ('grp', 'inner'))  76.7 us
    another operation x2, other arithmetic  67.1 us
    all_gather x1, waiting for transfers between devices, shards(): wide = lax.all_gather(local, 'inner', axis=3, tiled=True)  51.2 us
    unnamed x70, local copies, waits for them, and re-layouts  43 us
    all_gather x1, local copies, waits for them, and re-layouts, shards(): wide = lax.all_gather(local, 'inner', axis=3, tiled=True)  32.9 us
    all_to_all x1, local copies, waits for them, and re-layouts, shards(): rows = lax.all_to_all(wide, 'grp', split_axis=3, concat_axis=0, tiled=True)  24.9 us
    dot_general x8, matrix products, shards(): jnp.dot(block, col_steer, precision=lax.Precision.HIGHEST, preferred_elem...  15.8 us
  transfers between devices with their start and end apart: 3, of which 1 were waited for; matrix products, arithmetic and copies ran while one was open for 35% of the time, Pallas kernels for 0%

commit v1 on v0

--- a/solution.py
+++ b/solution.py
@@ -82,7 +82,7 @@
         )
         partial_value.append(jnp.sum(row_steer * image, axis=0))
     partial_value = jnp.stack(partial_value, 0)
-    total = lax.psum(partial_value, ("grp", "inner"))
+    total = jnp.sum(lax.all_gather(partial_value, ("grp", "inner")), axis=0)
     return total * (math.sqrt(snaps) / total_mics)
 
 

time: 353 us -> 700 us (1.98)
  waiting for transfers between devices: 51.9 us -> 471 us
  blocking collectives: 76.7 us -> 0 us
    all_gather x0 -> x1, waiting for transfers between devices: none -> 419 us  [shards(): total = jnp.sum(lax.all_gather(partial_value, ('grp', 'inner')), axis=0)]
    psum x1 -> x0, blocking collectives: 76.7 us -> none  [shards(): total = lax.psum(partial_value, ('grp', 'inner'))]
  transfers between devices with their start and end apart: 3 -> 4, of which waited for: 1 -> 2; matrix products, arithmetic and copies ran while one was open for 35% -> 18% of each run, Pallas kernels for 0% -> 0%
where the time goes in v1:
time: 700 us; the launch traced here: 695 us
  waiting for transfers between devices  471 us (67%)
  local copies, waits for them, and re-layouts  104 us (15%)
  other arithmetic  72.6 us (10%)
  matrix products  20.9 us (3%)
  between operations  18.7 us (3%)
  starting transfers between devices  7.07 us (1%)
    all_gather x1, waiting for transfers between devices, shards(): total = jnp.sum(lax.all_gather(partial_value, ('grp', 'inner')), axis=0)  419 us
    another operation x2, other arithmetic  67.1 us
    all_gather x1, waiting for transfers between devices, shards(): wide = lax.all_gather(local, 'inner', axis=3, tiled=True)  51.2 us
    unnamed x70, local copies, waits for them, and re-layouts  43 us
    all_gather x1, local copies, waits for them, and re-layouts, shards(): wide = lax.all_gather(local, 'inner', axis=3, tiled=True)  32.9 us
    all_to_all x1, local copies, waits for them, and re-layouts, shards(): rows = lax.all_to_all(wide, 'grp', split_axis=3, concat_axis=0, tiled=True)  24.9 us
    dot_general x8, matrix products, shards(): jnp.dot(block, col_steer, precision=lax.Precision.HIGHEST, preferred_elem...  15.8 us
  transfers between devices with their start and end apart: 4, of which 2 were waited for; matrix products, arithmetic and copies ran while one was open for 18% of the time, Pallas kernels for 0%

profile of v1, /device:TPU:1, one launch (start us, length us, event | category | flops | bytes accessed | tf_op | source)
XLA Modules:
  0.0 694.8 jit_solution(10848533065960447674)
XLA Ops:
  6.5 0.0 all-gather.5.cloned.1.call-start
  6.6 0.9 multiply_convert_fusion.1
  7.5 3.5 fusion
  10.9 0.0 all-gather.5.cloned.1.call-update
  11.0 0.0 all-gather.7.cloned.1.call-start
  11.0 0.7 all-gather.7.cloned.1.call-update
  11.7 51.2 %all-gather.5.cloned.1.call-done = bf16[8,2,8,4096]{3,2,1,0:T(8,128)(2,1)} async-done(((bf16[8,2,8,256]{3,2,1,0:T(8,128)(2,1)}), bf16[8,2,8,4096]{3,2,1,0:T(8,128)(2,1)}) %all-gather.5.cloned.1.call-update) | async-done | bytes 1048592 | tf_op jit(solution)/shard_map/all_gather | solution.py:51
  62.9 32.9 %copy.15 = bf16[8,2,8,4096]{2,1,0,3:T(2,128)(2,1)} copy(bf16[8,2,8,4096]{3,2,1,0:T(8,128)(2,1)} %all-gather.5.cloned.1.call-done) | data formatting | bytes 2097152 | tf_op jit(solution)/shard_map/all_gather | solution.py:51
  95.8 20.6 %reshape.89 = bf16[16,2,16384]{2,1,0:T(2,128)(2,1)} reshape(bf16[4096,8,2,8]{3,2,1,0:T(2,128)(2,1)} %bitcast.131) | data formatting | bytes 2097152
  116.5 7.0 %all-to-all-start = ((bf16[16,2,16384]{2,1,0:T(2,128)(2,1)}), bf16[16,2,16384]{2,1,0:T(2,128)(2,1)S(1)}, u32[]{:S(2)}, u32[]{:S(2)}) async-start(bf16[16,2,16384]{2,1,0:T(2,128)(2,1)} %reshape.89), calls=%async_computation | async-start | bytes 2097152 | tf_op jit(solution)/shard_map/all_to_all | solution.py:52
  123.5 0.0 all-gather.9.cloned.1.call-start
  123.5 0.0 copy-done
  123.5 0.7 fusion.139
  129.2 0.9 constant_dynamic-slice_fusion.1
  130.1 0.0 copy-done.1
  130.1 66.3 %cosine_convert_fusion = (bf16[256,1024]{1,0:T(8,128)(2,1)}, bf16[256,1024]{1,0:T(8,128)(2,1)S(1)}, bf16[256,1024]{1,0:T(8,128)(2,1)}, bf16[256,1024]{1,0:T(8,12...) fusion(f32[]{:T(128)} %bitcast.49, ...), kind=kLoop, calls=%fused_computation.110 | loop fusion | flops 20971520 | bytes 16795680 | tf_op jit(solution)/shard_map/convert
  196.4 0.0 all-gather.7.cloned.1.call-done
  196.4 1.3 fusion.137
  197.7 0.4 copy.20
  198.2 0.4 copy.19
  198.6 0.0 all-to-all-done
  198.6 20.8 %reshape.90 = bf16[4096,8,2,8]{3,2,1,0:T(2,128)(2,1)} reshape(bf16[16,2,16384]{2,1,0:T(2,128)(2,1)S(1)} %all-to-all-done) | data formatting | bytes 2097152
  219.4 24.9 %copy.16 = bf16[8,2,8,16,256]{4,0,3,2,1:T(8,128)(2,1)S(1)} copy(bf16[8,2,8,16,256]{2,1,0,4,3:T(2,128)(2,1)} %bitcast.132) | data formatting | bytes 2097152 | tf_op jit(solution)/shard_map/all_to_all | solution.py:52
  244.3 0.4 fusion.83
  244.7 0.4 fusion.85
  245.1 0.4 convolution_add_fusion
  245.6 0.4 convolution_subtract_fusion
  246.0 0.0 copy-start.29
  246.0 0.0 copy-start.30
  246.0 0.0 copy-start.31
  246.0 0.8 fusion.129
  246.9 0.2 copy-done.29
  247.0 0.2 copy-done.30
  247.2 0.2 copy-done.31
  247.4 0.2 copy-done.32
  247.5 1.9 multiply_reduce_fusion.1
  249.6 1.9 multiply_reduce_fusion.2
  251.5 0.0 copy-done.21
  251.5 0.0 copy-done.22
  251.5 0.0 copy-done.23
  251.5 0.0 copy-done.24
  251.6 0.0 copy-start.17
  251.6 0.0 copy-start.18
  251.6 0.0 copy-start.19
  251.6 0.0 copy-start.20
  251.6 1.9 multiply_reduce_fusion.3
  253.6 1.9 multiply_reduce_fusion.4
  255.6 0.0 copy-done.13
  255.6 0.0 copy-done.14
  255.6 0.0 copy-done.15
  255.6 0.0 copy-done.16
  255.6 0.0 copy-start.9
  255.6 0.0 copy-start.10
  255.6 0.0 copy-start.11
  255.6 0.0 copy-start.12
  255.6 1.9 multiply_reduce_fusion.5
  257.7 2.2 multiply_reduce_fusion.6
  259.9 1.9 multiply_reduce_fusion
  261.9 1.9 multiply_reduce_fusion.7
  263.8 0.7 stack.35
  264.5 0.0 all-gather.9.cloned.1.call-update
  264.5 419.2 %all-gather.9.cloned.1.call-done = f32[2048,1024]{1,0:T(8,128)} async-done(((f32[8,1024]{1,0:T(8,128)}), f32[2048,1024]{1,0:T(8,128)}) %all-gather.9.cloned.1.call-update) | async-done | bytes 8388624 | tf_op jit(solution)/shard_map/all_gather | solution.py:85
  683.8 3.9 bitcast_reduce_fusion
  687.7 0.6 broadcast_multiply_fusion
  (44 shorter events, 0.1 us)
Async XLA Ops:
  6.5 56.4 %all-gather.5.cloned.1.call-start = ((), (), s32[]{:S(2)}) async-start(), calls=%async_computation.1 | async-start | bytes 1114112 | tf_op jit(solution)/shard_map/all_gather | solution.py:51
  11.0 185.5 %all-gather.7.cloned.1.call-start = ((), (), s32[]{:S(2)}) async-start(), calls=%async_computation.2 | async-start | bytes 1114112 | tf_op jit(solution)/shard_map/all_gather | solution.py:58
  116.5 7.1 %copy-start = (s32[8]{0:T(128)S(1)}, s32[8]{0:T(128)}, u32[]{:S(2)}) copy-start(s32[8]{0:T(128)} %param.5) | copy-start | bytes 100
  116.5 13.7 %copy-start.1 = (f32[3,1024]{1,0:T(4,128)S(1)}, f32[3,1024]{1,0:T(4,128)}, u32[]{:S(2)}) copy-start(f32[3,1024]{1,0:T(4,128)} %param.7) | copy-start | bytes 36868
  116.5 82.1 %all-to-all-start = ((bf16[16,2,16384]{2,1,0:T(2,128)(2,1)}), bf16[16,2,16384]{2,1,0:T(2,128)(2,1)S(1)}, u32[]{:S(2)}, u32[]{:S(2)}) async-start(bf16[16,2,16384]{2,1,0:T(2,128)(2,1)} %reshape.89), calls=%async_computation | async-start | bytes 2097152 | tf_op jit(solution)/shard_map/all_to_all | solution.py:52
  123.5 560.3 %all-gather.9.cloned.1.call-start = ((), (), s32[]{:S(2)}) async-start(), calls=%async_computation.3 | async-start | bytes 8421376 | tf_op jit(solution)/shard_map/all_gather | solution.py:85
  246.0 1.0 copy-start.29
  246.0 1.2 copy-start.30
  246.0 1.3 copy-start.31
  246.0 1.5 copy-start.32
  247.5 2.0 copy-start.25
  247.5 2.0 copy-start.26
  247.5 2.0 copy-start.27
  247.5 2.0 copy-start.28
  249.5 2.0 copy-start.21
  249.5 2.0 copy-start.22
  249.5 2.0 copy-start.23
  249.5 2.0 copy-start.24
  251.6 2.0 copy-start.17
  251.6 2.0 copy-start.18
  251.6 2.0 copy-start.19
  251.6 2.0 copy-start.20
  253.6 2.0 copy-start.13
  253.6 2.0 copy-start.14
  253.6 2.0 copy-start.15
  253.6 2.0 copy-start.16
  255.6 2.0 copy-start.9
  255.6 2.0 copy-start.10
  255.6 2.0 copy-start.11
  255.6 2.0 copy-start.12
  257.6 2.2 copy-start.5
  257.6 2.2 copy-start.6
  257.7 2.2 copy-start.7
  257.7 2.2 copy-start.8
  259.9 2.0 copy-start.2
  259.9 2.0 copy-start.3
  259.9 2.0 copy-start.4
Sparse Core Ops, SparseCore 0:
  11.1 51.7 all-gather.4
  64.7 57.6 all-gather.6
  264.7 419.0 all-gather.8
